TPU v7x, 32 devices: a whole 2x2x4 slice. The times are simulated.
32 devices in a mesh: dp: 8 (over z, x), fsdp: 4 (over y, core).
Axes of the slice: x: 2, y: 2, z: 4, core: 2. Of those that a mesh axis runs over, the one named last changes fastest.
Arguments:
- tokens: float32 [16, 1024, 512], P('dp', 'fsdp'), may hold values from -12 to 12
- segments: int32 [16, 1024], P('dp', 'fsdp'), may hold values from 0 to 15, never falling along the last dimension, each value on 1 to 512 neighbouring positions
- cotangent: float32 [16, 1024, 512], P('dp', 'fsdp'), may hold values from -6 to 6
- ln1_gain: float32 [512], P('dp'), may hold values from 0.5 to 1.5
- ln1_bias: float32 [512], P('dp'), may hold values from -2.5 to 2.5
- w_qkv: float32 [512, 1536], P('fsdp', 'dp'), may hold values from -0.25 to 0.25
- w_out: float32 [512, 512], P('fsdp', 'dp'), may hold values from -1.5 to 1.5
- ln2_gain: float32 [512], P('dp'), may hold values from 0.5 to 1.5
- ln2_bias: float32 [512], P('dp'), may hold values from -2.5 to 2.5
- w_up: float32 [512, 2048], P('fsdp', 'dp'), may hold values from -0.25 to 0.25
- w_down: float32 [2048, 512], P('fsdp', 'dp'), may hold values from -0.125 to 0.125
Outputs:
- output: float32 [16, 1024, 512], P('dp', 'fsdp')
- grad_tokens: float32 [16, 1024, 512], P('dp', 'fsdp')
- grad_ln1_gain: float32 [512], P('dp')
- grad_ln1_bias: float32 [512], P('dp')
- grad_w_qkv: float32 [512, 1536], P('fsdp', 'dp')
- grad_w_out: float32 [512, 512], P('fsdp', 'dp')
- grad_ln2_gain: float32 [512], P('dp')
- grad_ln2_bias: float32 [512], P('dp')
- grad_w_up: float32 [512, 2048], P('fsdp', 'dp')
- grad_w_down: float32 [2048, 512], P('fsdp', 'dp')
Inputs may be any that keep to these rules, and one draw needn't show every extreme that they name: `segments`: in each sequence the numbers never fall; each document runs for 1 to 512 tokens, and one runs for exactly 512.
All inputs are finite; a program needn't handle non-finite values.
Results may differ from a plain program's by a relative error of at most 0.0003.
Values sent between devices are 32-bit elements; how exact they have to be, the bound alone decides.
No kernel may reach another device: no remote copies, remote signals or barrier semaphores. Data moves between devices by JAX's collectives and lax.ppermute only.
A program may use at most 256 MiB of HBM per device.

v0:
```python
import jax
import jax.numpy as jnp
from jax import lax
from jax.sharding import PartitionSpec as P

D = 512
HEADS = 8
NR = 16
LEVELS = 6
MICRO = 2


EPSILON = 1e-05
MASKED = -1e30
HIGHEST = lax.Precision.HIGHEST


def layer_norm(values, gain_vec, shift_vec):
    centre = values - jnp.mean(values, axis=-1, keepdims=True)
    spread = jnp.mean(centre * centre, axis=-1, keepdims=True)
    return centre * lax.rsqrt(spread + EPSILON) * gain_vec + shift_vec


def coarsen(values, group_ratio):
    batch_size, item_count, head_count, head_width = values.shape
    return jnp.mean(
        values.reshape(batch_size, item_count // group_ratio, group_ratio, head_count, head_width),
        axis=2,
    )


def seg_range(seg_block, group_ratio):
    batch_size, item_count = seg_block.shape
    grouped = seg_block.reshape(batch_size, item_count // group_ratio, group_ratio)
    return (jnp.min(grouped, axis=2), jnp.max(grouped, axis=2))


def sibling(values):
    full_shape = values.shape
    paired = values.reshape((full_shape[0], full_shape[1] // 2, 2) + full_shape[2:])
    return jnp.flip(paired, axis=2).reshape(full_shape)


def expand(values, group_ratio):
    return jnp.repeat(values, group_ratio, axis=1)


def block_part(queries, key_heads, val_heads, low_query, high_query, low_key, high_key, swapped):
    batch_size, item_count, head_count, head_width = queries.shape
    blocks = item_count // NR
    query_b = queries.reshape(batch_size, blocks, NR, head_count, head_width)
    key_b = key_heads.reshape(batch_size, blocks, NR, head_count, head_width)
    val_b = val_heads.reshape(batch_size, blocks, NR, head_count, head_width)
    low_qb = low_query.reshape(batch_size, blocks, NR)
    high_qb = high_query.reshape(batch_size, blocks, NR)
    low_kb = low_key.reshape(batch_size, blocks, NR)
    high_kb = high_key.reshape(batch_size, blocks, NR)
    if swapped:
        key_b = sibling(key_b)
        val_b = sibling(val_b)
        low_kb = sibling(low_kb)
        high_kb = sibling(high_kb)
    scores = jnp.einsum("gbihd,gbjhd->gbhij", query_b, key_b, precision=HIGHEST) * head_width ** (
        -0.5
    )
    allowed = (low_qb[..., :, None] <= high_kb[..., None, :]) & (
        low_kb[..., None, :] <= high_qb[..., :, None]
    )
    scores = jnp.where(allowed[:, :, None], scores, MASKED)
    peak_score = jnp.max(scores, axis=-1)
    probabilities = jnp.exp(scores - peak_score[..., None])
    weight_sum = jnp.sum(probabilities, axis=-1)
    mixture = jnp.einsum("gbhij,gbjhd->gbihd", probabilities, val_b, precision=HIGHEST)
    peak_score = jnp.swapaxes(peak_score, 2, 3).reshape(batch_size, item_count, head_count)
    weight_sum = jnp.swapaxes(weight_sum, 2, 3).reshape(batch_size, item_count, head_count)
    return (peak_score, weight_sum, mixture.reshape(batch_size, item_count, head_count, head_width))


def key_part(queries, key_heads, val_heads, low_query, high_query, low_key, high_key):
    scores = jnp.einsum("gihd,gjhd->ghij", queries, key_heads, precision=HIGHEST) * queries.shape[
        -1
    ] ** (-0.5)
    allowed = (low_query[:, :, None] <= high_key[:, None, :]) & (
        low_key[:, None, :] <= high_query[:, :, None]
    )
    scores = jnp.where(allowed[:, None], scores, MASKED)
    peak_score = jnp.max(scores, axis=-1)
    probabilities = jnp.exp(scores - peak_score[..., None])
    weight_sum = jnp.sum(probabilities, axis=-1)
    mixture = jnp.einsum("ghij,gjhd->gihd", probabilities, val_heads, precision=HIGHEST)
    return (jnp.swapaxes(peak_score, 1, 2), jnp.swapaxes(weight_sum, 1, 2), mixture)


def combine(part_list):
    overall = part_list[0][0]
    for part_item in part_list[1:]:
        overall = jnp.maximum(overall, part_item[0])
    denominator = jnp.zeros_like(overall)
    numerator = jnp.zeros_like(part_list[0][2])
    for peak_score, weight_sum, mixture, group_ratio in part_list:
        factor = group_ratio * jnp.exp(peak_score - overall)
        denominator = denominator + factor * weight_sum
        numerator = numerator + factor[..., None] * mixture
    return numerator / denominator[..., None]


def coarse_sends(packed, crossing):
    batch_size, shard_len, triple = packed.shape
    model_width = triple // 3
    split_heads = packed.reshape(batch_size, shard_len, 3, HEADS, model_width // HEADS)
    key_list = [
        coarsen(split_heads[:, :, 1], 2**level_index).reshape(batch_size, -1, model_width)
        for level_index in crossing
    ]
    val_list = [
        coarsen(split_heads[:, :, 2], 2**level_index).reshape(batch_size, -1, model_width)
        for level_index in crossing
    ]
    return (jnp.concatenate(key_list, axis=1), jnp.concatenate(val_list, axis=1))


def local_attention(
    packed, far_keys, far_vals, seg_local, seg_whole, position, shard_count, local_levels, crossing
):
    batch_size, shard_len, triple = packed.shape
    model_width = triple // 3
    head_width = model_width // HEADS
    split_heads = packed.reshape(batch_size, shard_len, 3, HEADS, head_width)
    queries = split_heads[:, :, 0]
    key_heads = split_heads[:, :, 1]
    val_heads = split_heads[:, :, 2]
    part_list = [
        block_part(queries, key_heads, val_heads, seg_local, seg_local, seg_local, seg_local, False)
        + (1.0,)
    ]
    for level_index in local_levels:
        group_ratio = 2**level_index
        low_group, high_group = seg_range(seg_local, group_ratio)
        peak_score, weight_sum, mixture = block_part(
            coarsen(queries, group_ratio),
            coarsen(key_heads, group_ratio),
            coarsen(val_heads, group_ratio),
            low_group,
            high_group,
            low_group,
            high_group,
            True,
        )
        part_list.append(
            (
                expand(peak_score, group_ratio),
                expand(weight_sum, group_ratio),
                expand(mixture, group_ratio),
                float(group_ratio),
            )
        )
    far_k = far_keys.reshape(batch_size, shard_count, -1, model_width)
    far_v = far_vals.reshape(batch_size, shard_count, -1, model_width)
    offset = 0
    for level_index in crossing:
        group_ratio = 2**level_index
        local_count = shard_len // group_ratio
        whole_k = far_k[:, :, offset : offset + local_count].reshape(
            batch_size, shard_count * local_count, HEADS, head_width
        )
        whole_v = far_v[:, :, offset : offset + local_count].reshape(
            batch_size, shard_count * local_count, HEADS, head_width
        )
        offset = offset + local_count
        first_coarse = position * local_count
        partner = jnp.bitwise_xor(first_coarse // NR, 1) * NR
        block_k = lax.dynamic_slice_in_dim(whole_k, partner, NR, 1)
        block_v = lax.dynamic_slice_in_dim(whole_v, partner, NR, 1)
        low_whole, high_whole = seg_range(seg_whole, group_ratio)
        low_key = lax.dynamic_slice_in_dim(low_whole, partner, NR, 1)
        high_key = lax.dynamic_slice_in_dim(high_whole, partner, NR, 1)
        low_query, high_query = seg_range(seg_local, group_ratio)
        peak_score, weight_sum, mixture = key_part(
            coarsen(queries, group_ratio),
            block_k,
            block_v,
            low_query,
            high_query,
            low_key,
            high_key,
        )
        part_list.append(
            (
                expand(peak_score, group_ratio),
                expand(weight_sum, group_ratio),
                expand(mixture, group_ratio),
                float(group_ratio),
            )
        )
    return combine(part_list).reshape(batch_size, shard_len, model_width)


def outer_sum(left, right):
    return lax.dot_general(left, right, (((0,), (0,)), ((), ())), precision=HIGHEST)


def back_mul(grad_rows, weight):
    return lax.dot_general(grad_rows, weight, (((1,), (1,)), ((), ())), precision=HIGHEST)


def fetch_forward(ln1_gain, ln1_bias, w_qkv, w_out, ln2_gain, ln2_bias, w_up, w_down):
    section_one = (
        lax.all_gather(w_qkv, "fsdp", axis=0, tiled=True),
        lax.all_gather(w_out, "fsdp", axis=0, tiled=True),
        lax.all_gather(w_up, "fsdp", axis=0, tiled=True),
        lax.all_gather(w_down, "fsdp", axis=0, tiled=True),
    )
    return (
        lax.all_gather(ln1_gain, "dp", axis=0, tiled=True),
        lax.all_gather(ln1_bias, "dp", axis=0, tiled=True),
        lax.all_gather(section_one[0], "dp", axis=1, tiled=True),
        lax.all_gather(section_one[1], "dp", axis=1, tiled=True),
        lax.all_gather(ln2_gain, "dp", axis=0, tiled=True),
        lax.all_gather(ln2_bias, "dp", axis=0, tiled=True),
        lax.all_gather(section_one[2], "dp", axis=1, tiled=True),
        lax.all_gather(section_one[3], "dp", axis=1, tiled=True),
    )


def fetch_backward(w_qkv, w_out, w_up, w_down):
    section_one = (
        lax.all_gather(w_qkv, "fsdp", axis=0, tiled=True),
        lax.all_gather(w_out, "fsdp", axis=0, tiled=True),
        lax.all_gather(w_up, "fsdp", axis=0, tiled=True),
        lax.all_gather(w_down, "fsdp", axis=0, tiled=True),
    )
    return (
        lax.all_gather(section_one[0], "dp", axis=1, tiled=True),
        lax.all_gather(section_one[1], "dp", axis=1, tiled=True),
        lax.all_gather(section_one[2], "dp", axis=1, tiled=True),
        lax.all_gather(section_one[3], "dp", axis=1, tiled=True),
    )


def local(
    tokens, segments, cotangent, ln1_gain, ln1_bias, w_qkv, w_out, ln2_gain, ln2_bias, w_up, w_down
):
    seq_count, shard_len, model_width = tokens.shape
    shard_count = lax.axis_size("fsdp")
    position = lax.axis_index("fsdp")
    crossing = [
        level_index for level_index in range(LEVELS) if NR * 2 ** (level_index + 1) > shard_len
    ]
    local_levels = [
        level_index for level_index in range(LEVELS) if NR * 2 ** (level_index + 1) <= shard_len
    ]
    seg_whole = lax.all_gather(segments, "fsdp", axis=1, tiled=True)
    acc_gain_one = jnp.zeros((D,), jnp.float32)
    acc_bias_one = jnp.zeros((D,), jnp.float32)
    acc_gain_two = jnp.zeros((D,), jnp.float32)
    acc_bias_two = jnp.zeros((D,), jnp.float32)
    micro_len = seq_count // MICRO
    flat_rows = micro_len * shard_len
    outputs = []
    input_grads = []
    kept_normed = []
    kept_packed_grad = []
    kept_mixture = []
    kept_middle_grad = []
    kept_normed_two = []
    kept_pre_grad = []
    kept_hidden = []
    kept_cot = []
    for micro_index in range(MICRO):
        start_row = micro_index * micro_len
        stop_row = start_row + micro_len
        micro_tokens = tokens[start_row:stop_row]
        seg_part = segments[start_row:stop_row]
        whole_part = seg_whole[start_row:stop_row]
        params = fetch_forward(ln1_gain, ln1_bias, w_qkv, w_out, ln2_gain, ln2_bias, w_up, w_down)
        gain_one, bias_one, full_qkv, full_out, gain_two, bias_two, full_up, full_down = params
        normed, ln_one_pull = jax.vjp(layer_norm, micro_tokens, gain_one, bias_one)
        normed_flat = normed.reshape(flat_rows, model_width)
        packed = jnp.dot(normed_flat, full_qkv, precision=HIGHEST).reshape(
            micro_len, shard_len, 3 * model_width
        )
        (send_k, send_v), send_pull = jax.vjp(lambda source: coarse_sends(source, crossing), packed)
        far_keys, far_vals = (
            lax.all_gather(send_k, "fsdp", axis=1, tiled=True),
            lax.all_gather(send_v, "fsdp", axis=1, tiled=True),
        )

        def attend(source, keys_in, vals_in):
            return local_attention(
                source,
                keys_in,
                vals_in,
                seg_part,
                whole_part,
                position,
                shard_count,
                local_levels,
                crossing,
            )

        mixture, attend_pull = jax.vjp(attend, packed, far_keys, far_vals)
        mixture_flat = mixture.reshape(flat_rows, model_width)
        middle = micro_tokens + jnp.dot(mixture_flat, full_out, precision=HIGHEST).reshape(
            micro_tokens.shape
        )
        normed_two, ln_two_pull = jax.vjp(layer_norm, middle, gain_two, bias_two)
        normed_two_flat = normed_two.reshape(flat_rows, model_width)
        hidden, gelu_pull = jax.vjp(
            jax.nn.gelu, jnp.dot(normed_two_flat, full_up, precision=HIGHEST)
        )
        output = middle + jnp.dot(hidden, full_down, precision=HIGHEST).reshape(micro_tokens.shape)
        outputs.append(output)
        back_qkv, back_out, back_up, back_down = fetch_backward(w_qkv, w_out, w_up, w_down)
        micro_cot = cotangent[start_row:stop_row]
        grad_flat = micro_cot.reshape(flat_rows, model_width)
        grad_hidden = back_mul(grad_flat, back_down)
        (grad_pre,) = gelu_pull(grad_hidden)
        grad_normed_two = back_mul(grad_pre, back_up).reshape(micro_tokens.shape)
        grad_middle, grad_gain_two, grad_bias_two = ln_two_pull(grad_normed_two)
        grad_middle = grad_middle + micro_cot
        acc_gain_two = acc_gain_two + grad_gain_two
        acc_bias_two = acc_bias_two + grad_bias_two
        middle_flat = grad_middle.reshape(flat_rows, model_width)
        grad_mixture = back_mul(middle_flat, back_out).reshape(mixture.shape)
        grad_packed, grad_far_k, grad_far_v = attend_pull(grad_mixture)
        grad_send_k, grad_send_v = (
            lax.psum_scatter(grad_far_k, "fsdp", scatter_dimension=1, tiled=True),
            lax.psum_scatter(grad_far_v, "fsdp", scatter_dimension=1, tiled=True),
        )
        (grad_extra,) = send_pull((grad_send_k, grad_send_v))
        packed_flat = (grad_packed + grad_extra).reshape(flat_rows, 3 * model_width)
        grad_normed = back_mul(packed_flat, back_qkv).reshape(micro_tokens.shape)
        grad_input, grad_gain_one, grad_bias_one = ln_one_pull(grad_normed)
        acc_gain_one = acc_gain_one + grad_gain_one
        acc_bias_one = acc_bias_one + grad_bias_one
        input_grads.append(grad_middle + grad_input)
        kept_normed.append(normed_flat)
        kept_packed_grad.append(packed_flat)
        kept_mixture.append(mixture_flat)
        kept_middle_grad.append(middle_flat)
        kept_normed_two.append(normed_two_flat)
        kept_pre_grad.append(grad_pre)
        kept_hidden.append(hidden)
        kept_cot.append(grad_flat)
    acc_qkv = outer_sum(
        jnp.concatenate(kept_normed, axis=0), jnp.concatenate(kept_packed_grad, axis=0)
    )
    acc_out = outer_sum(
        jnp.concatenate(kept_mixture, axis=0), jnp.concatenate(kept_middle_grad, axis=0)
    )
    acc_up = outer_sum(
        jnp.concatenate(kept_normed_two, axis=0), jnp.concatenate(kept_pre_grad, axis=0)
    )
    acc_down = outer_sum(jnp.concatenate(kept_hidden, axis=0), jnp.concatenate(kept_cot, axis=0))
    reduced = (
        lax.psum_scatter(acc_qkv, "dp", scatter_dimension=1, tiled=True),
        lax.psum_scatter(acc_out, "dp", scatter_dimension=1, tiled=True),
        lax.psum_scatter(acc_up, "dp", scatter_dimension=1, tiled=True),
        lax.psum_scatter(acc_down, "dp", scatter_dimension=1, tiled=True),
        lax.psum_scatter(acc_gain_one, "dp", scatter_dimension=0, tiled=True),
        lax.psum_scatter(acc_bias_one, "dp", scatter_dimension=0, tiled=True),
        lax.psum_scatter(acc_gain_two, "dp", scatter_dimension=0, tiled=True),
        lax.psum_scatter(acc_bias_two, "dp", scatter_dimension=0, tiled=True),
    )
    matrices = (
        lax.psum_scatter(reduced[0], "fsdp", scatter_dimension=0, tiled=True),
        lax.psum_scatter(reduced[1], "fsdp", scatter_dimension=0, tiled=True),
        lax.psum_scatter(reduced[2], "fsdp", scatter_dimension=0, tiled=True),
        lax.psum_scatter(reduced[3], "fsdp", scatter_dimension=0, tiled=True),
    )
    norm_parts = lax.psum((reduced[4], reduced[5], reduced[6], reduced[7]), "fsdp")
    return (
        jnp.concatenate(outputs, axis=0),
        jnp.concatenate(input_grads, axis=0),
        norm_parts[0],
        norm_parts[1],
        matrices[0],
        matrices[1],
        norm_parts[2],
        norm_parts[3],
        matrices[2],
        matrices[3],
    )


def solution(mesh):
    return jax.shard_map(
        local,
        mesh=mesh,
        in_specs=(
            P("dp", "fsdp", None),
            P("dp", "fsdp"),
            P("dp", "fsdp", None),
            P("dp"),
            P("dp"),
            P("fsdp", "dp"),
            P("fsdp", "dp"),
            P("dp"),
            P("dp"),
            P("fsdp", "dp"),
            P("fsdp", "dp"),
        ),
        out_specs=(
            P("dp", "fsdp", None),
            P("dp", "fsdp", None),
            P("dp"),
            P("dp"),
            P("fsdp", "dp"),
            P("fsdp", "dp"),
            P("dp"),
            P("dp"),
            P("fsdp", "dp"),
            P("fsdp", "dp"),
        ),
        check_vma=False,
    )
```

profile of v0, /device:TPU:0, one launch (start us, length us, event | category | flops | bytes accessed | tf_op | source)
XLA Modules:
  0.0 1648.3 jit_solution(8584037883864069647)
XLA Ops:
  7.3 9.6 all_gather.36
  17.0 6.1 all_gather.41
  23.2 9.1 all_gather.90
  32.4 7.8 all_gather.92
  40.3 5.2 all_gather.38
  55.9 23.0 %all-reduce.31 = (f32[512]{0:T(512)S(1)}, f32[512]{0:T(512)S(1)}, f32[512]{0:T(512)}, f32[512]{0:T(512)}) all-reduce(f32[512]{0:T(512)S(1)} %dynamic-update-slice.1, f32[512]{0:T(512)S(1)} %dynamic-update-slice, f32[512]{0:T(512)S(1)} %dynamic-update-slice.3, f32[512]{0:T(512)S(1)} %dynamic-update-slice.2), channel_id=1, replica_groups=mesh['dp'=8,'fsdp'=4] {'dp'}, use_global_device_ids=true, to_apply=%add.23 | all-reduce | flops 2048 | bytes 16384
  83.7 4.7 convolution_bitcast_fusion
  90.1 5.6 all_gather.95
  97.8 5.8 all_gather.94
  118.1 5.6 all_gather.40
  126.8 6.0 all_gather.39
  166.2 3.4 fusion.654
  250.5 3.3 fusion.661
  374.2 3.5 convolution_bitcast_fusion.10
  463.0 3.5 convolution_bitcast_fusion.12
  498.2 3.6 fusion.663
  730.1 8.2 multiply_multiply_fusion.4
  738.4 7.8 fusion.23
  746.3 4.7 fusion.132
  751.0 5.3 multiply_multiply_fusion.5
  756.4 4.7 fusion.17
  761.2 4.5 fusion.641
  791.0 3.9 multiply_reduce_fusion.2
  838.1 5.4 fusion.672
  877.5 4.4 fusion.675
  892.8 4.1 add_reduce_fusion
  978.7 3.9 multiply_reduce_fusion.14
  1021.0 5.4 fusion.665
  1060.4 4.4 fusion.668
  1075.7 4.0 add_reduce_fusion.2
  1154.4 3.3 fusion.90
  1159.5 4.5 convolution_bitcast_fusion.3
  1169.0 4.4 convolution_bitcast_fusion.7
  1244.5 3.6 copy.5367
  1248.1 4.4 fusion.679
  1257.3 6.8 fusion.8
  1266.0 9.9 fusion
  1277.7 9.8 fusion.4
  1288.3 74.5 %reduce-scatter.21.cloned.1.call-done = f32[512,192]{0,1:T(8,128)} async-done(((f32[512,1536]{0,1:T(8,128)}), f32[512,192]{0,1:T(8,128)}) %reduce-scatter.21.cloned.1.call-update) | async-done | bytes 393232 | tf_op jit(solution)/shard_map/reduce_scatter | solution.py:356
  1362.8 91.6 %reduce-scatter.29.cloned.1.call-done = f32[512,256]{1,0:T(8,128)} async-done(((f32[512,2048]{1,0:T(8,128)}), f32[512,256]{1,0:T(8,128)}) %reduce-scatter.29.cloned.1.call-update) | async-done | bytes 524304 | tf_op jit(solution)/shard_map/reduce_scatter | solution.py:358
  1456.7 7.4 fusion.41
  1464.1 5.1 fusion.39
  1469.2 76.4 %reduce-scatter.33.cloned.1.call-done = f32[2048,64]{0,1:T(8,128)} async-done(((f32[2048,512]{0,1:T(8,128)}), f32[2048,64]{0,1:T(8,128)}) %reduce-scatter.33.cloned.1.call-update) | async-done | bytes 524304 | tf_op jit(solution)/shard_map/reduce_scatter | solution.py:359
  1548.0 20.4 %all-reduce.30 = (f32[512]{0:T(512)S(1)}, f32[512]{0:T(512)S(1)}, f32[512]{0:T(512)S(1)}, f32[512]{0:T(512)S(1)}) all-reduce(f32[512]{0:T(512)S(1)} %add.886, f32[512]{0:T(512)S(1)} %add.887, f32[512]{0:T(512)S(1)} %add.888, f32[512]{0:T(512)S(1)} %add.889), channel_id=6, replica_groups=mesh['dp'=8,'fsdp'=4] {'dp'}, use_global_device_ids=true, to_apply=%region_190.191.clone | all-reduce | flops 2048 | bytes 16384
  1568.7 6.1 all-reduce.32
  1577.6 14.4 reduce-scatter.23.cloned.1.call-done
  1591.9 24.6 %reduce-scatter.31.cloned.1.call-done = f32[128,256]{1,0:T(8,128)} async-done(((f32[512,256]{1,0:T(8,128)}), f32[128,256]{1,0:T(8,128)}) %reduce-scatter.31.cloned.1.call-update) | async-done | bytes 131088 | tf_op jit(solution)/shard_map/reduce_scatter | solution.py:368
  1616.5 24.8 %reduce-scatter.35.cloned.1.call-done = f32[512,64]{0,1:T(8,128)} async-done(((f32[2048,64]{0,1:T(8,128)}), f32[512,64]{0,1:T(8,128)}) %reduce-scatter.35.cloned.1.call-update) | async-done | bytes 131088 | tf_op jit(solution)/shard_map/reduce_scatter | solution.py:369
  (2103 shorter events, 1057.2 us)
Async XLA Ops:
  7.2 25.2 %copy-start.442 = (f32[512,64]{0,1:T(8,128)S(1)}, f32[512,64]{0,1:T(8,128)}, u32[]{:S(2)}) copy-start(f32[512,64]{0,1:T(8,128)} %param.21) | copy-start | bytes 393220
  7.2 33.1 %copy-start.528 = (s32[2,256]{1,0:T(2,128)S(1)}, s32[2,256]{1,0:T(2,128)}, u32[]{:S(2)}) copy-start(s32[2,256]{1,0:T(2,128)} %param.12) | copy-start | bytes 6148
  7.2 41.9 %copy-start.8 = (f32[2,256,512]{2,1,0:T(8,128)S(1)}, f32[2,256,512]{2,1,0:T(8,128)}, u32[]{:S(2)}) copy-start(f32[2,256,512]{2,1,0:T(8,128)} %param.11) | copy-start | bytes 3145732
  7.2 76.5 %all-gather.5.cloned.1.call-start = ((), (), s32[]{:S(2)}) async-start(), calls=%async_computation.12 | async-start | bytes 3538944 | tf_op jit(solution)/shard_map/all_gather | solution.py:216
  16.9 481.2 %all-gather.7.cloned.1.call-start = ((), (), s32[]{:S(2)}) async-start(), calls=%async_computation.13 | async-start | bytes 1179648 | tf_op jit(solution)/shard_map/all_gather | solution.py:217
  23.1 707.0 %all-gather.9.cloned.1.call-start = ((), (), s32[]{:S(2)}) async-start(), calls=%async_computation.14 | async-start | bytes 4718592 | tf_op jit(solution)/shard_map/all_gather | solution.py:220
  32.4 706.0 %all-gather.11.cloned.1.call-start = ((), (), s32[]{:S(2)}) async-start(), calls=%async_computation.15 | async-start | bytes 4718592 | tf_op jit(solution)/shard_map/all_gather | solution.py:221
  40.2 1189.2 %reduce-scatter.19.cloned.1.call-start = ((), (), s32[]{:S(2)}) async-start(), calls=%async_computation.19 | async-start | bytes 245760 | tf_op jit(solution)/shard_map/reduce_scatter | solution.py:327
  49.3 39.1 %copy-start.488 = (f32[256]{0:T(256)}, f32[256]{0:T(256)S(1)}, u32[]{:S(2)}) copy-start(f32[256]{0:T(256)S(1)} %get-tuple-element.303) | copy-start | bytes 3076
  49.3 63.9 %copy-start.490 = (f32[256]{0:T(256)}, f32[256]{0:T(256)S(1)}, u32[]{:S(2)}) copy-start(f32[256]{0:T(256)S(1)} %get-tuple-element.304) | copy-start | bytes 3076
  49.6 38.8 %copy-start.521 = (f32[256]{0:T(256)}, f32[256]{0:T(256)S(1)}, u32[]{:S(2)}) copy-start(f32[256]{0:T(256)S(1)} %get-tuple-element.46) | copy-start | bytes 3076
  49.6 38.8 %copy-start.505 = (f32[256]{0:T(256)}, f32[256]{0:T(256)S(1)}, u32[]{:S(2)}) copy-start(f32[256]{0:T(256)S(1)} %fusion.558) | copy-start | bytes 3076
  51.3 61.9 %copy-start.507 = (f32[256]{0:T(256)}, f32[256]{0:T(256)S(1)}, u32[]{:S(2)}) copy-start(f32[256]{0:T(256)S(1)} %fusion.556) | copy-start | bytes 3076
  55.2 51.2 %copy-start.328 = (pred[16,16,16]{1,2,0:T(8,128)(4,1)}, pred[16,16,16]{1,2,0:T(8,128)(4,1)S(1)}, u32[]{:S(2)}) copy-start(pred[16,16,16]{1,2,0:T(8,128)(4,1)S(1)} %get-tuple-element.223) | copy-start | bytes 12292
  55.9 79.7 %copy-start.326 = (pred[16,16,16]{1,2,0:T(8,128)(4,1)}, pred[16,16,16]{1,2,0:T(8,128)(4,1)S(1)}, u32[]{:S(2)}) copy-start(pred[16,16,16]{1,2,0:T(8,128)(4,1)S(1)} %get-tuple-element.220) | copy-start | bytes 12292
  78.9 34.4 %copy-start.454 = (f32[512]{0:T(512)}, f32[512]{0:T(512)S(1)}, u32[]{:S(2)}) copy-start(f32[512]{0:T(512)S(1)} %get-tuple-element.97) | copy-start | bytes 6148
  78.9 34.4 %copy-start.509 = (f32[512]{0:T(512)}, f32[512]{0:T(512)S(1)}, u32[]{:S(2)}) copy-start(f32[512]{0:T(512)S(1)} %get-tuple-element.96) | copy-start | bytes 6148
  80.2 125.1 %copy-start.481 = (pred[2,16,16]{1,2,0:T(8,128)(4,1)}, pred[2,16,16]{1,2,0:T(8,128)(4,1)S(1)}, u32[]{:S(2)}) copy-start(pred[2,16,16]{1,2,0:T(8,128)(4,1)S(1)} %compare_and_fusion.8) | copy-start | bytes 1540
  80.3 76.6 %copy-start.441 = (pred[4,16,16]{1,2,0:T(8,128)(4,1)}, pred[4,16,16]{1,2,0:T(8,128)(4,1)S(1)}, u32[]{:S(2)}) copy-start(pred[4,16,16]{1,2,0:T(8,128)(4,1)S(1)} %compare_and_fusion.6) | copy-start | bytes 3076
  80.4 68.1 %copy-start.378 = (pred[8,16,16]{1,2,0:T(8,128)(4,1)}, pred[8,16,16]{1,2,0:T(8,128)(4,1)S(1)}, u32[]{:S(2)}) copy-start(pred[8,16,16]{1,2,0:T(8,128)(4,1)S(1)} %compare_and_fusion.4) | copy-start | bytes 6148
  108.5 72.7 %copy-start.58 = (f32[16,8,16]{2,1,0:T(8,128)}, f32[16,8,16]{2,1,0:T(8,128)S(1)}, u32[]{:S(2)}) copy-start(f32[16,8,16]{2,1,0:T(8,128)S(1)} %get-tuple-element.246) | copy-start | bytes 24580
  137.7 127.8 %copy-start.55 = (f32[16,8,16]{2,1,0:T(8,128)}, f32[16,8,16]{2,1,0:T(8,128)S(1)}, u32[]{:S(2)}) copy-start(f32[16,8,16]{2,1,0:T(8,128)S(1)} %get-tuple-element.260) | copy-start | bytes 24580
  159.2 192.5 %copy-start.66 = (f32[4,8,16,16]{2,3,1,0:T(8,128)}, f32[4,8,16,16]{2,3,1,0:T(8,128)S(1)}, u32[]{:S(2)}) copy-start(f32[4,8,16,16]{2,3,1,0:T(8,128)S(1)} %get-tuple-element.241) | copy-start | bytes 98308
  206.6 23.8 %copy-start.370 = (f32[2,8,16]{2,1,0:T(8,128)}, f32[2,8,16]{2,1,0:T(8,128)S(1)}, u32[]{:S(2)}) copy-start(f32[2,8,16]{2,1,0:T(8,128)S(1)} %get-tuple-element.238) | copy-start | bytes 3076
  291.4 32.1 %copy-start.164 = (f32[32,8,8]{1,0,2:T(8,128)}, f32[32,8,8]{1,0,2:T(8,128)S(1)}, u32[]{:S(2)}) copy-start(f32[32,8,8]{1,0,2:T(8,128)S(1)} %broadcast_in_dim.1413.clone) | copy-start | bytes 24580
  1131.1 99.9 %reduce-scatter.17.cloned.1.call-start = ((), (), s32[]{:S(2)}) async-start(), calls=%async_computation.18 | async-start | bytes 245760 | tf_op jit(solution)/shard_map/reduce_scatter | solution.py:328
  1157.7 77.3 %reduce-scatter.15.cloned.1.call-start = ((), (), s32[]{:S(2)}) async-start(), calls=%async_computation.17 | async-start | bytes 245760 | tf_op jit(solution)/shard_map/reduce_scatter | solution.py:327
  1167.2 68.5 %reduce-scatter.13.cloned.1.call-start = ((), (), s32[]{:S(2)}) async-start(), calls=%async_computation.16 | async-start | bytes 245760 | tf_op jit(solution)/shard_map/reduce_scatter | solution.py:328
  1176.5 111.1 %reduce-scatter.25.cloned.1.call-start = ((), (), s32[]{:S(2)}) async-start(), calls=%async_computation.22 | async-start | bytes 1179648 | tf_op jit(solution)/shard_map/reduce_scatter | solution.py:357
  1211.3 151.4 %reduce-scatter.21.cloned.1.call-start = ((), (), s32[]{:S(2)}) async-start(), calls=%async_computation.20 | async-start | bytes 3538944 | tf_op jit(solution)/shard_map/reduce_scatter | solution.py:356
  1264.2 190.3 %reduce-scatter.29.cloned.1.call-start = ((), (), s32[]{:S(2)}) async-start(), calls=%async_computation.24 | async-start | bytes 4718592 | tf_op jit(solution)/shard_map/reduce_scatter | solution.py:358
  1275.9 269.8 %reduce-scatter.33.cloned.1.call-start = ((), (), s32[]{:S(2)}) async-start(), calls=%async_computation.26 | async-start | bytes 4718592 | tf_op jit(solution)/shard_map/reduce_scatter | solution.py:359
  1287.4 168.0 %copy-start.87 = (f32[256,512]{1,0:T(8,128)S(1)}, f32[256,512]{1,0:T(8,128)}, u32[]{:S(2)}) copy-start(f32[256,512]{1,0:T(8,128)} %copy-done.86) | copy-start | bytes 1572868
  1287.4 169.2 %copy-start.42 = (f32[256,2048]{1,0:T(8,128)S(1)}, f32[256,2048]{1,0:T(8,128)}, u32[]{:S(2)}) copy-start(f32[256,2048]{1,0:T(8,128)} %get-tuple-element.300) | copy-start | bytes 6291460
  1287.4 169.2 %copy-start.527 = (f32[512]{0:T(512)S(1)}, f32[512]{0:T(512)}, u32[]{:S(2)}) copy-start(f32[512]{0:T(512)} %get-tuple-element.229) | copy-start | bytes 6148
  1287.5 169.2 %copy-start.529 = (f32[512]{0:T(512)S(1)}, f32[512]{0:T(512)}, u32[]{:S(2)}) copy-start(f32[512]{0:T(512)} %get-tuple-element.42) | copy-start | bytes 6148
  1287.5 169.2 %copy-start.19 = (f32[1,256,512]{2,1,0:T(8,128)S(1)}, f32[1,256,512]{2,1,0:T(8,128)}, u32[]{:S(2)}) copy-start(f32[1,256,512]{2,1,0:T(8,128)} %get-tuple-element.265) | copy-start | bytes 1572868
  1287.5 290.1 %reduce-scatter.27.cloned.1.call-start = ((), (), s32[]{:S(2)}) async-start(), calls=%async_computation.23 | async-start | bytes 163840 | tf_op jit(solution)/shard_map/reduce_scatter | solution.py:367
  1288.2 303.7 %reduce-scatter.23.cloned.1.call-start = ((), (), s32[]{:S(2)}) async-start(), calls=%async_computation.21 | async-start | bytes 491520 | tf_op jit(solution)/shard_map/reduce_scatter | solution.py:366
  1362.8 253.8 %reduce-scatter.31.cloned.1.call-start = ((), (), s32[]{:S(2)}) async-start(), calls=%async_computation.25 | async-start | bytes 655360 | tf_op jit(solution)/shard_map/reduce_scatter | solution.py:368
  1454.5 186.8 %reduce-scatter.35.cloned.1.call-start = ((), (), s32[]{:S(2)}) async-start(), calls=%async_computation.27 | async-start | bytes 655360 | tf_op jit(solution)/shard_map/reduce_scatter | solution.py:369
  1469.2 78.8 %copy-start.50 = (f32[256,512]{1,0:T(8,128)S(1)}, f32[256,512]{1,0:T(8,128)}, u32[]{:S(2)}) copy-start(f32[256,512]{1,0:T(8,128)} %copy-done.49) | copy-start | bytes 1572868
  1469.2 105.7 %copy-start.12 = (f32[2,256,512]{2,1,0:T(8,128)S(1)}, f32[2,256,512]{2,1,0:T(8,128)}, u32[]{:S(2)}) copy-start(f32[2,256,512]{2,1,0:T(8,128)} %param.11) | copy-start | bytes 3145732
  1469.2 105.7 %copy-start.46 = (f32[256,512]{1,0:T(8,128)S(1)}, f32[256,512]{1,0:T(8,128)}, u32[]{:S(2)}) copy-start(f32[256,512]{1,0:T(8,128)} %copy-done.45) | copy-start | bytes 1572868
  1469.2 105.7 %copy-start.110 = (f32[1,256,512]{2,1,0:T(8,128)S(1)}, f32[1,256,512]{2,1,0:T(8,128)}, u32[]{:S(2)}) copy-start(f32[1,256,512]{2,1,0:T(8,128)} %copy-done.109) | copy-start | bytes 1572868
  1469.2 105.7 %copy-start.112 = (f32[1,256,512]{2,1,0:T(8,128)S(1)}, f32[1,256,512]{2,1,0:T(8,128)}, u32[]{:S(2)}) copy-start(f32[1,256,512]{2,1,0:T(8,128)} %copy-done.111) | copy-start | bytes 1572868
  1469.2 105.7 %copy-start.524 = (f32[256]{0:T(256)S(1)}, f32[256]{0:T(256)}, u32[]{:S(2)}) copy-start(f32[256]{0:T(256)} %copy-done.523) | copy-start | bytes 3076
  1469.2 105.7 %copy-start.526 = (f32[256]{0:T(256)S(1)}, f32[256]{0:T(256)}, u32[]{:S(2)}) copy-start(f32[256]{0:T(256)} %copy-done.525) | copy-start | bytes 3076
  (504 other events, 2775.9 us)
Sparse Core Ops, SparseCore 0:
  17.0 61.6 all-gather.4
  80.8 38.9 all-gather.6
  121.9 73.8 all-gather.8
  197.8 71.5 all-gather.10
  1131.3 16.1 reduce-scatter.18
  1157.8 16.1 reduce-scatter.16
  1176.4 19.7 reduce-scatter.14
  1198.7 19.7 reduce-scatter.12
  1221.8 63.4 reduce-scatter.24
  1289.1 73.5 reduce-scatter.20
  1366.8 87.5 reduce-scatter.28
  1457.9 87.6 reduce-scatter.32
  1548.8 19.3 reduce-scatter.26
  1571.1 20.8 reduce-scatter.22
  1594.8 21.6 reduce-scatter.30
  1619.6 21.6 reduce-scatter.34
where the time goes:
time: 1670 us; the launch traced here: 1650 us
  local copies, waits for them, and re-layouts  673 us (40%)
  waiting for transfers between devices  307 us (18%)
  matrix products  278 us (17%)
  other arithmetic  255 us (15%)
  blocking collectives  110 us (7%)
  between operations  22.8 us (1%)
    broadcast_in_dim x190, local copies, waits for them, and re-layouts, expand(): return jnp.repeat(values, group_ratio, axis=1)  208 us
    reduce_scatter x1, waiting for transfers between devices, local(): lax.psum_scatter(acc_up, 'dp', scatter_dimension=1, tiled=True)  91.6 us
    reduce_scatter x1, waiting for transfers between devices, local(): lax.psum_scatter(acc_down, 'dp', scatter_dimension=1, tiled=True)  76.4 us
    reduce_scatter x1, waiting for transfers between devices, local(): lax.psum_scatter(acc_qkv, 'dp', scatter_dimension=1, tiled=True)  74.5 us
    dot_general x30, matrix products, block_part(): jnp.einsum('gbhij,gbjhd->gbihd', probabilities, val_b, precision=HIGHEST)  69.9 us
    dot_general x30, matrix products, block_part(): jnp.einsum('gbihd,gbjhd->gbhij', query_b, key_b, precision=HIGHEST)  67.3 us
    reduce_sum x30, other arithmetic, expand(): return jnp.repeat(values, group_ratio, axis=1)  62.7 us
    broadcast_in_dim x38, local copies, waits for them, and re-layouts, combine(): numerator = numerator + factor[..., None] * mixture  57.9 us
  transfers between devices with their start and end apart: 16, of which 6 were waited for; matrix products, arithmetic and copies ran while one was open for 47% of the time, Pallas kernels for 0%

commit v1 on v0

v1 whole, which is shorter than its diff:
```python
import jax
import jax.numpy as jnp
import numpy as np
from jax import lax
from jax.experimental import pallas as pl
from jax.experimental.pallas import tpu as pltpu
from jax.sharding import PartitionSpec as P

HEADS = 8
NR = 16
LEVELS = 6
EPSILON = 1e-05
MASKED = -1e30
F32 = jnp.float32
BF16 = jnp.bfloat16
LN_ROWS = 16


def split(x):
    high = x.astype(BF16)
    return high, (x - high.astype(F32)).astype(BF16)


def mm(a, b, ca, cb):
    return lax.dot_general(a, b, (((ca,), (cb,)), ((), ())), preferred_element_type=F32)


def mm3(a, b, ca, cb):
    return mm(a[0], b[0], ca, cb) + mm(a[0], b[1], ca, cb) + mm(a[1], b[0], ca, cb)


def mm2(a, b, ca, cb):
    return mm(a, b[0], ca, cb) + mm(a, b[1], ca, cb)


def level_layout(length):
    rows, start = [], 0
    for level in range(1, LEVELS):
        count = length >> level
        rows.append((level, start, count))
        start += count
    return rows, start


def pooling(length):
    spread = np.zeros((length, length), np.float32)
    pool = np.zeros((length, length), np.float32)
    same = np.zeros((length, length), np.float32)
    layout, _ = level_layout(length)
    bounds = [first for _, first, _ in layout] + [length]
    for index, (level, first, count) in enumerate(layout):
        token = np.arange(length)
        spread[token, first + (token >> level)] = 1.0
        pool[first + (token >> level), token] = 0.5**level
        same[bounds[index] : bounds[index + 1], bounds[index] : bounds[index + 1]] = 1.0
    return spread, pool, same


def score_bias(seg, near, far_a, far_b):
    count, length = seg.shape
    token = np.arange(length)
    pair = (token[:, None] >> 5) == (token[None, :] >> 5)
    ok = pair[None] & (seg[:, :, None] == seg[:, None, :])
    parts = [jnp.where(ok, 0.0, MASKED)]
    for level in range(1, LEVELS):
        ratio = 1 << level

        def ends(values):
            grouped = values.reshape(count, length // ratio, ratio)
            return grouped[:, :, 0], grouped[:, :, -1]

        low_q, high_q = ends(seg)
        low_q = jnp.repeat(low_q, ratio, axis=1)
        high_q = jnp.repeat(high_q, ratio, axis=1)
        if 2 * NR * ratio <= length:
            low_k, high_k = ends(seg)
            block_q = (token >> level) >> 4
            block_k = np.arange(length >> level) >> 4
            where = (block_q[:, None] ^ 1) == block_k[None, :]
        else:
            if NR * ratio <= length:
                low_k, high_k = ends(near)
            else:
                pieces = [ends(far_a), ends(far_b)]
                low_k = jnp.concatenate([pieces[0][0], pieces[1][0]], axis=1)
                high_k = jnp.concatenate([pieces[0][1], pieces[1][1]], axis=1)
            where = np.ones((length, low_k.shape[1]), bool)
        ok = (
            where[None]
            & (low_q[:, :, None] <= high_k[:, None, :])
            & (low_k[:, None, :] <= high_q[:, :, None])
        )
        parts.append(jnp.where(ok, np.float32(level * np.log(2.0)), MASKED))
    return jnp.concatenate(parts, axis=2).astype(F32)


class Plan:
    def __init__(self, dp, fsdp):
        self.dp, self.fsdp = dp, fsdp

    def slots(self):
        return [(d, f) for d in range(self.dp) for f in range(self.fsdp)]


def assemble(scratch, refs, plan, me_d, me_f, rows, lanes):
    for d, f in plan.slots():
        row = pl.multiple_of((me_d ^ d) * rows, 8)
        col = pl.multiple_of((me_f ^ f) * lanes, 128)
        scratch[pl.ds(row, rows), pl.ds(col, lanes)] = refs[0][d, f, :rows, :]


def norm_rows(refs, plan, rows):
    total = refs[0][0, 0, rows:, :]
    for d in range(1, plan.dp):
        total = total + refs[0][d, 0, rows:, :]
    return jnp.concatenate([total[4 * i : 4 * i + 4] for i in range(4)], axis=1)


def whole(shape=None):
    return pl.BlockSpec(memory_space=pltpu.VMEM)


SMEM = pl.BlockSpec(memory_space=pltpu.SMEM)


def call(body, outs, scratch=(), **kw):
    return pl.pallas_call(
        body,
        out_shape=[jax.ShapeDtypeStruct(s, t) for s, t in outs],
        scratch_shapes=list(scratch),
        **kw,
    )


def qkv_stage(me, tokens, slots, plan, pool, seqs):
    rows_all, width = tokens.shape
    length = rows_all // seqs
    triple = 3 * width
    rows = triple // plan.dp
    lanes = width // plan.fsdp
    n4, n5 = length >> 4, length >> 5

    def body(me_ref, tok, pool_ref, *rest):
        refs = rest[: len(slots)]
        packed, wh, wl, xhat, inv, ln, s4, s5, full = rest[len(slots) :]
        assemble(full, refs, plan, me_ref[0], me_ref[1], rows, lanes)
        params = norm_rows(refs, plan, rows)
        ln[0:4, :] = params
        w = split(full[...])
        wh[...] = w[0]
        wl[...] = w[1]
        x = tok[...]
        centre = x - jnp.mean(x, axis=1, keepdims=True)
        scale = lax.rsqrt(jnp.mean(centre * centre, axis=1, keepdims=True) + EPSILON)
        xh = centre * scale
        xhat[...] = xh
        inv[...] = jnp.broadcast_to(scale, inv.shape)
        normed = xh * params[0:1, :] + params[1:2, :]
        packed[...] = mm3(split(normed), w, 1, 1)
        a24 = pool_ref[...]
        for s in range(seqs):
            for j in range(2):
                kv = packed[
                    s * length : (s + 1) * length, (j + 1) * width : (j + 2) * width
                ]
                means = mm2(a24, split(kv), 1, 0)
                s4[s, j] = means[:n4]
                s5[s, j] = means[n4 : n4 + n5]

    return call(
        body,
        [
            ((rows_all, triple), F32),
            ((triple, width), BF16),
            ((triple, width), BF16),
            ((rows_all, width), F32),
            ((rows_all, 128), F32),
            ((8, width), F32),
            ((seqs, 2, n4, width), F32),
            ((seqs, 2, n5, width), F32),
        ],
        [pltpu.VMEM((triple, width), F32)],
        in_specs=[SMEM, whole(), whole()] + [whole()] * len(slots),
        out_specs=[whole()] * 8,
    )(me, tokens, pool, *slots)


def head_tools(q, k, v, fk, fv, pool, same, local):
    length = q.shape[0]
    lane = lax.broadcasted_iota(jnp.int32, (length, 128), 1) < 64
    pooled = mm2(pool, split(jnp.concatenate([q, k, v], axis=1)), 1, 0)
    qc = pooled[:, :128]
    kc = jnp.concatenate([pooled[:local, 128:256], fk], axis=0)
    vc = jnp.concatenate([pooled[:local, 256:], fv], axis=0)

    def both(x):
        zero = jnp.zeros_like(x)
        return jnp.concatenate([jnp.where(lane, x, zero), jnp.where(lane, zero, x)], axis=0)

    return lane, both, split(both(q)), split(k), split(v), split(both(qc)), split(kc), split(vc)


def pair_scores(q2, ks, qc2, kcs, spread, same, bias):
    length = spread.shape[0]
    s0 = mm3(q2, ks, 1, 1)
    sc = mm3(qc2, kcs, 1, 1) * jnp.concatenate([same, same], axis=0)
    sch, scl = split(sc)
    st = jnp.concatenate(
        [
            mm2(spread, (sch[:length], scl[:length]), 1, 0),
            mm2(spread, (sch[length:], scl[length:]), 1, 0),
        ],
        axis=0,
    )
    b0 = bias[:, :length]
    bc = bias[:, length:]
    return s0 + jnp.concatenate([b0, b0], axis=0), st + jnp.concatenate([bc, bc], axis=0)


def attention_specs(length, width):
    pairs = width // 128
    block = lambda off: pl.BlockSpec((length, 128), lambda s, h: (s, off * pairs + h))
    far = lambda j: pl.BlockSpec((1, 1, 32, 128), lambda s, h: (s, j, 0, h))
    fixed = pl.BlockSpec((length, length), lambda s, h: (0, 0))
    bias = pl.BlockSpec((1, length, 2 * length), lambda s, h: (s, 0, 0))
    return block, far, fixed, bias


def attention_forward(packed, far, bias, spread, pool, same, seqs, local):
    rows_all, triple = packed.shape
    width = triple // 3
    length = rows_all // seqs
    block, far_spec, fixed, bias_spec = attention_specs(length, width)

    def body(q_ref, k_ref, v_ref, fk, fv, bias_ref, spread_ref, pool_ref, same_ref, out, lse):
        lane, both, q2, ks, vs, qc2, kcs, vcs = head_tools(
            q_ref[...] * 0.125,
            k_ref[...],
            v_ref[...],
            fk[0, 0],
            fv[0, 0],
            pool_ref[...],
            same_ref[...],
            local,
        )
        s0, st = pair_scores(q2, ks, qc2, kcs, spread_ref[...], same_ref[...], bias_ref[0])
        peak = jnp.maximum(
            jnp.max(s0, axis=1, keepdims=True), jnp.max(st, axis=1, keepdims=True)
        )
        p0 = jnp.exp(s0 - peak)
        pc = jnp.exp(st - peak)
        total = jnp.sum(p0, axis=1, keepdims=True) + jnp.sum(pc, axis=1, keepdims=True)
        mixed = (mm3(split(p0), vs, 1, 0) + mm3(split(pc), vcs, 1, 0)) / total
        out[...] = jnp.where(lane, mixed[:length], mixed[length:])
        logs = peak + jnp.log(total)
        lse[...] = jnp.where(lane, logs[:length], logs[length:])

    return pl.pallas_call(
        body,
        grid=(seqs, width // 128),
        out_shape=[jax.ShapeDtypeStruct((rows_all, width), F32)] * 2,
        in_specs=[
            block(0),
            block(1),
            block(2),
            far_spec(0),
            far_spec(1),
            bias_spec,
            fixed,
            fixed,
            fixed,
        ],
        out_specs=[block(0), block(0)],
    )(packed, packed, packed, far, far, bias, spread, pool, same)


def attention_backward(packed, far, bias, spread, pool, same, attended, lse, grad, seqs, local):
    rows_all, triple = packed.shape
    width = triple // 3
    length = rows_all // seqs
    block, far_spec, fixed, bias_spec = attention_specs(length, width)
    n4, n5 = length >> 4, length >> 5

    def body(
        q_ref,
        k_ref,
        v_ref,
        fk,
        fv,
        bias_ref,
        spread_ref,
        pool_ref,
        same_ref,
        o_ref,
        lse_ref,
        g_ref,
        dq_ref,
        dk_ref,
        dv_ref,
        f4,
        f5a,
        f5b,
    ):
        pool_m = pool_ref[...]
        spread_m = spread_ref[...]
        lane, both, q2, ks, vs, qc2, kcs, vcs = head_tools(
            q_ref[...] * 0.125,
            k_ref[...],
            v_ref[...],
            fk[0, 0],
            fv[0, 0],
            pool_m,
            same_ref[...],
            local,
        )
        s0, st = pair_scores(q2, ks, qc2, kcs, spread_m, same_ref[...], bias_ref[0])
        logs = lse_ref[...]
        logs2 = jnp.concatenate([logs[:, 0:1], logs[:, 64:65]], axis=0)
        p0 = jnp.exp(s0 - logs2)
        pc = jnp.exp(st - logs2)
        g2f = both(g_ref[...])
        g2 = split(g2f)
        o_val = o_ref[...]
        delta = jnp.sum(g2f * jnp.concatenate([o_val, o_val], axis=0), axis=1, keepdims=True)
        dv = mm3(split(p0), g2, 0, 0)
        dvc = mm3(split(pc), g2, 0, 0)
        d0 = split(p0 * (mm3(g2, vs, 1, 1) - delta))
        dt = split(pc * (mm3(g2, vcs, 1, 1) - delta))
        dq2 = mm3(d0, ks, 1, 0)
        dk = mm3(d0, q2, 0, 0)
        dsc = jnp.concatenate(
            [
                mm2_left((dt[0][:length], dt[1][:length]), spread_m),
                mm2_left((dt[0][length:], dt[1][length:]), spread_m),
            ],
            axis=0,
        )
        dsc = split(dsc * jnp.concatenate([same_ref[...], same_ref[...]], axis=0))
        dqc2 = mm3(dsc, kcs, 1, 0)
        dkc = mm3(dsc, qc2, 0, 0)
        dqc = jnp.where(lane, dqc2[:length], dqc2[length:])
        near = lax.broadcasted_iota(jnp.int32, (length, 128), 0) < local
        zero = jnp.zeros((length, 128), F32)
        stacked = jnp.concatenate(
            [dqc, jnp.where(near, dkc, zero), jnp.where(near, dvc, zero)], axis=1
        )
        back = mm2(pool_m, split(stacked), 0, 0)
        dq_ref[...] = (jnp.where(lane, dq2[:length], dq2[length:]) + back[:, :128]) * 0.125
        dk_ref[...] = dk + back[:, 128:256]
        dv_ref[...] = dv + back[:, 256:]
        for j, value in ((0, dkc), (1, dvc)):
            f4[0, j] = value[local : local + n4]
            f5a[0, j] = value[local + n4 : local + n4 + n5]
            f5b[0, j] = value[local + n4 + n5 :]

    far_out = lambda n: pl.BlockSpec((1, 2, n, 128), lambda s, h: (s, 0, 0, h))
    return pl.pallas_call(
        body,
        grid=(seqs, width // 128),
        out_shape=[jax.ShapeDtypeStruct((rows_all, width), F32)] * 3
        + [jax.ShapeDtypeStruct((seqs, 2, n, width), F32) for n in (n4, n5, n5)],
        in_specs=[
            block(0),
            block(1),
            block(2),
            far_spec(0),
            far_spec(1),
            bias_spec,
            fixed,
            fixed,
            fixed,
            block(0),
            block(0),
            block(0),
        ],
        out_specs=[block(0)] * 3 + [far_out(n4), far_out(n5), far_out(n5)],
    )(packed, packed, packed, far, far, bias, spread, pool, same, attended, lse, grad)


def mm2_left(a, b):
    return mm(b, a[0], 0, 0) + mm(b, a[1], 0, 0)


def middle_stage(me, tokens, attended, slots, plan):
    rows_all, width = tokens.shape
    rows, lanes = width // plan.dp, width // plan.fsdp

    def body(me_ref, tok, att, *rest):
        refs = rest[: len(slots)]
        middle, xhat, inv, wh, wl, full = rest[len(slots) :]
        assemble(full, refs, plan, me_ref[0], me_ref[1], rows, lanes)
        w = split(full[...])
        wh[...] = w[0]
        wl[...] = w[1]
        x = tok[...] + mm3(split(att[...]), w, 1, 1)
        middle[...] = x
        centre = x - jnp.mean(x, axis=1, keepdims=True)
        scale = lax.rsqrt(jnp.mean(centre * centre, axis=1, keepdims=True) + EPSILON)
        xhat[...] = centre * scale
        inv[...] = jnp.broadcast_to(scale, inv.shape)

    return call(
        body,
        [
            ((rows_all, width), F32),
            ((rows_all, width), F32),
            ((rows_all, 128), F32),
            ((width, width), BF16),
            ((width, width), BF16),
        ],
        [pltpu.VMEM((width, width), F32)],
        in_specs=[SMEM, whole(), whole()] + [whole()] * len(slots),
        out_specs=[whole()] * 5,
    )(me, tokens, attended, *slots)


def grad_hidden_stage(me, cot, slots, plan, hidden_width):
    rows_all, width = cot.shape
    rows, lanes = width // plan.dp, hidden_width // plan.fsdp

    def body(me_ref, cot_ref, *rest):
        refs = rest[: len(slots)]
        gh, wh, wl, full = rest[len(slots) :]
        assemble(full, refs, plan, me_ref[0], me_ref[1], rows, lanes)
        w = split(full[...])
        wh[...] = w[0]
        wl[...] = w[1]
        gh[...] = mm3(split(cot_ref[...]), w, 1, 0)

    return call(
        body,
        [
            ((rows_all, hidden_width), F32),
            ((width, hidden_width), BF16),
            ((width, hidden_width), BF16),
        ],
        [pltpu.VMEM((width, hidden_width), F32)],
        in_specs=[SMEM, whole()] + [whole()] * len(slots),
        out_specs=[whole()] * 3,
    )(me, cot, *slots)


def hidden_stage(me, xhat, ln, gh, slots, plan):
    rows_all, width = xhat.shape
    hidden_width = gh.shape[1]
    rows, lanes = hidden_width // plan.dp, width // plan.fsdp
    chunk = 512
    steps = hidden_width // chunk
    root = float(np.sqrt(2.0 / np.pi))

    def body(me_ref, xhat_ref, ln_ref, gh_ref, *rest):
        refs = rest[: len(slots)]
        hh, hl, ph, plo, wh, wl, full, nh, nl = rest[len(slots) :]
        step = pl.program_id(0)

        @pl.when(step == 0)
        def _():
            assemble(full, refs, plan, me_ref[0], me_ref[1], rows, lanes)
            w = split(full[...])
            wh[...] = w[0]
            wl[...] = w[1]
            n = split(xhat_ref[...] * ln_ref[2:3, :] + ln_ref[3:4, :])
            nh[...] = n[0]
            nl[...] = n[1]

        part = pl.ds(pl.multiple_of(step * chunk, chunk), chunk)
        v = mm3((nh[...], nl[...]), (wh[part, :], wl[part, :]), 1, 1)
        square = v * v
        t = jnp.tanh(root * v * (1.0 + 0.044715 * square))
        half = 0.5 * (1.0 + t)
        h = split(v * half)
        hh[...] = h[0]
        hl[...] = h[1]
        slope = half + 0.5 * v * (1.0 - t * t) * root * (1.0 + 3 * 0.044715 * square)
        g = split(gh_ref[...] * slope)
        ph[...] = g[0]
        plo[...] = g[1]

    fixed = lambda shape: pl.BlockSpec(shape, lambda i: (0,) * len(shape))
    cols = pl.BlockSpec((rows_all, chunk), lambda i: (0, i))
    return pl.pallas_call(
        body,
        grid=(steps,),
        out_shape=[jax.ShapeDtypeStruct((rows_all, hidden_width), BF16)] * 4
        + [jax.ShapeDtypeStruct((hidden_width, width), BF16)] * 2,
        in_specs=[SMEM, fixed((rows_all, width)), fixed((8, width)), cols]
        + [fixed(s.shape) for s in slots],
        out_specs=[cols] * 4 + [fixed((hidden_width, width))] * 2,
        scratch_shapes=[
            pltpu.VMEM((hidden_width, width), F32),
            pltpu.VMEM((rows_all, width), BF16),
            pltpu.VMEM((rows_all, width), BF16),
        ],
    )(me, xhat, ln, gh, *slots)


def grad_down_stage(me, cot, hh, hl, plan):
    rows_all, width = cot.shape
    hidden_width = hh.shape[1]
    rows, lanes = width // plan.dp, hidden_width // plan.fsdp

    def body(me_ref, cot_ref, hh_ref, hl_ref, out):
        res = mm3(split(cot_ref[...]), (hh_ref[...], hl_ref[...]), 0, 0)
        for d in range(plan.dp):
            out[d ^ me_ref[0], 0] = res[d * rows : (d + 1) * rows, :]

    grid_spec = pltpu.PrefetchScalarGridSpec(
        num_scalar_prefetch=1,
        grid=(plan.fsdp,),
        in_specs=[
            pl.BlockSpec((rows_all, width), lambda i, m: (0, 0)),
            pl.BlockSpec((rows_all, lanes), lambda i, m: (0, m[1] ^ i)),
            pl.BlockSpec((rows_all, lanes), lambda i, m: (0, m[1] ^ i)),
        ],
        out_specs=pl.BlockSpec((plan.dp, 1, rows, lanes), lambda i, m: (0, i, 0, 0)),
    )
    return pl.pallas_call(
        body,
        grid_spec=grid_spec,
        out_shape=jax.ShapeDtypeStruct((plan.dp, plan.fsdp, rows, lanes), F32),
    )(me, cot, hh, hl)


def grad_up_stage(me, xhat, ln, ph, plo, plan):
    rows_all, width = xhat.shape
    hidden_width = ph.shape[1]
    rows, lanes = hidden_width // plan.dp, width // plan.fsdp
    chunk = 512
    steps = hidden_width // chunk
    per = chunk // rows

    def body(me_ref, xhat_ref, ln_ref, ph_ref, pl_ref, out, nh, nl):
        step = pl.program_id(0)

        @pl.when(step == 0)
        def _():
            n = split(xhat_ref[...] * ln_ref[2:3, :] + ln_ref[3:4, :])
            nh[...] = n[0]
            nl[...] = n[1]

        res = mm3((ph_ref[...], pl_ref[...]), (nh[...], nl[...]), 0, 0)
        for i in range(per):
            for f in range(plan.fsdp):
                d = step * per + i
                out[d ^ me_ref[0], f ^ me_ref[1]] = res[
                    i * rows : (i + 1) * rows, f * lanes : (f + 1) * lanes
                ]

    fixed = lambda shape: pl.BlockSpec(shape, lambda i: (0,) * len(shape))
    cols = pl.BlockSpec((rows_all, chunk), lambda i: (0, i))
    shape = (plan.dp, plan.fsdp, rows, lanes)
    return pl.pallas_call(
        body,
        grid=(steps,),
        out_shape=jax.ShapeDtypeStruct(shape, F32),
        in_specs=[SMEM, fixed((rows_all, width)), fixed((8, width)), cols, cols],
        out_specs=fixed(shape),
        scratch_shapes=[pltpu.VMEM((rows_all, width), BF16)] * 2,
    )(me, xhat, ln, ph, plo)


def norm_back(e, gain, xhat, inv):
    u = e * gain
    mean_u = jnp.mean(u, axis=1, keepdims=True)
    mean_ux = jnp.mean(u * xhat, axis=1, keepdims=True)
    return inv * (u - mean_u - xhat * mean_ux)


def output_stage(middle, cot, xhat, inv, ln, hh, hl, ph, plo, dh, dl, uh, ul):
    rows_all, width = middle.shape
    hidden_width = hh.shape[1]
    chunk = 512
    steps = hidden_width // chunk

    def body(mid, cot_ref, xhat_ref, inv_ref, ln_ref, h0, h1, p0, p1, d0, d1, u0, u1, out, gm, gln, acc):
        step = pl.program_id(0)

        @pl.when(step == 0)
        def _():
            out[...] = mid[...]
            acc[...] = jnp.zeros_like(acc)

        out[...] += mm3((h0[...], h1[...]), (d0[...], d1[...]), 1, 1)
        acc[...] += mm3((p0[...], p1[...]), (u0[...], u1[...]), 1, 0)

        @pl.when(step == steps - 1)
        def _():
            e = acc[...]
            xh = xhat_ref[...]
            gm[...] = cot_ref[...] + norm_back(e, ln_ref[2:3, :], xh, inv_ref[:, 0:1])
            gln[0:1, :] = jnp.sum(e * xh, axis=0, keepdims=True)
            gln[1:2, :] = jnp.sum(e, axis=0, keepdims=True)

    fixed = lambda shape: pl.BlockSpec(shape, lambda i: (0,) * len(shape))
    cols = pl.BlockSpec((rows_all, chunk), lambda i: (0, i))
    act = fixed((rows_all, width))
    return pl.pallas_call(
        body,
        grid=(steps,),
        out_shape=[
            jax.ShapeDtypeStruct((rows_all, width), F32),
            jax.ShapeDtypeStruct((rows_all, width), F32),
            jax.ShapeDtypeStruct((8, width), F32),
        ],
        in_specs=[act, act, act, fixed((rows_all, 128)), fixed((8, width))]
        + [cols] * 4
        + [pl.BlockSpec((width, chunk), lambda i: (0, i))] * 2
        + [pl.BlockSpec((chunk, width), lambda i: (i, 0))] * 2,
        out_specs=[act, act, fixed((8, width))],
        scratch_shapes=[pltpu.VMEM((rows_all, width), F32)],
    )(middle, cot, xhat, inv, ln, hh, hl, ph, plo, dh, dl, uh, ul)


def mixture_grad_stage(me, gm, attended, oh, ol, plan):
    rows_all, width = gm.shape
    rows, lanes = width // plan.dp, width // plan.fsdp

    def body(me_ref, gm_ref, att, oh_ref, ol_ref, gmix, out):
        g = split(gm_ref[...])
        gmix[...] = mm3(g, (oh_ref[...], ol_ref[...]), 1, 0)
        res = mm3(g, split(att[...]), 0, 0)
        for d in range(plan.dp):
            for f in range(plan.fsdp):
                out[d ^ me_ref[0], f ^ me_ref[1]] = res[
                    d * rows : (d + 1) * rows, f * lanes : (f + 1) * lanes
                ]

    return call(
        body,
        [((rows_all, width), F32), ((plan.dp, plan.fsdp, rows, lanes), F32)],
        in_specs=[SMEM] + [whole()] * 4,
        out_specs=[whole()] * 2,
    )(me, gm, attended, oh, ol)


def input_grad_stage(dq, dk, dv, g4, g5a, g5b, pool, wqh, wql, xhat, inv, ln, gm, gln, seqs):
    rows_all, width = dq.shape
    length = rows_all // seqs

    def body(dq_r, dk_r, dv_r, g4_r, g5a_r, g5b_r, pool_r, wh, wl, xhat_r, inv_r, ln_r, gm_r, gln_r, gph, gpl, gtok, lrow):
        for j, ref in ((0, None), (1, dk_r), (2, dv_r)):
            for s in range(seqs):
                rs = slice(s * length, (s + 1) * length)
                if j == 0:
                    value = dq_r[rs, :]
                else:
                    groups = jnp.concatenate(
                        [g4_r[s, j - 1], g5a_r[s, j - 1] + g5b_r[s, j - 1]], axis=0
                    )
                    value = ref[rs, :] + mm2(pool_r[...], split(groups), 0, 0)
                h = split(value)
                gph[rs, j * width : (j + 1) * width] = h[0]
                gpl[rs, j * width : (j + 1) * width] = h[1]
        e = mm3((gph[...], gpl[...]), (wh[...], wl[...]), 1, 0)
        xh = xhat_r[...]
        gtok[...] = gm_r[...] + norm_back(e, ln_r[0:1, :], xh, inv_r[:, 0:1])
        sums = [
            jnp.sum(e * xh, axis=0, keepdims=True),
            jnp.sum(e, axis=0, keepdims=True),
            gln_r[0:1, :],
            gln_r[1:2, :],
        ]
        for i in range(4):
            for p in range(4):
                lrow[4 * i + p : 4 * i + p + 1, :] = sums[p][:, 128 * i : 128 * (i + 1)]

    return call(
        body,
        [
            ((rows_all, 3 * width), BF16),
            ((rows_all, 3 * width), BF16),
            ((rows_all, width), F32),
            ((LN_ROWS, 128), F32),
        ],
        in_specs=[whole()] * 14,
        out_specs=[whole()] * 4,
    )(dq, dk, dv, g4, g5a, g5b, pool, wqh, wql, xhat, inv, ln, gm, gln)


def grad_qkv_stage(me, gph, gpl, xhat, ln, lrow, plan):
    rows_all, triple = gph.shape
    width = triple // 3
    rows, lanes = triple // plan.dp, width // plan.fsdp

    def body(me_ref, gph_r, gpl_r, xhat_r, ln_r, lrow_r, out):
        n = split(xhat_r[...] * ln_r[0:1, :] + ln_r[1:2, :])
        res = mm3((gph_r[...], gpl_r[...]), n, 0, 0)
        tail = lrow_r[...]
        for d in range(plan.dp):
            for f in range(plan.fsdp):
                out[d ^ me_ref[0], f ^ me_ref[1], :rows, :] = res[
                    d * rows : (d + 1) * rows, f * lanes : (f + 1) * lanes
                ]
                out[d, f, rows:, :] = tail

    return call(
        body,
        [((plan.dp, plan.fsdp, rows + LN_ROWS, lanes), F32)],
        in_specs=[SMEM] + [whole()] * 5,
        out_specs=[whole()],
    )(me, gph, gpl, xhat, ln, lrow)[0]


def swap(x, mask, axis="fsdp"):
    size = lax.axis_size(axis)
    return lax.ppermute(x, axis, [(i, i ^ mask) for i in range(size)])


def gather(piece, plan):
    out = lax.all_gather(piece, ("dp", "fsdp"), axis=0, tiled=False)
    return [out.reshape((plan.dp, plan.fsdp) + piece.shape)]


def reduce_pieces(pieces, plan):
    flat = pieces.reshape((plan.dp * plan.fsdp,) + pieces.shape[2:])
    return lax.psum_scatter(flat, ("dp", "fsdp"), scatter_dimension=0, tiled=False)


def local(
    tokens, segments, cotangent, ln1_gain, ln1_bias, w_qkv, w_out, ln2_gain, ln2_bias, w_up, w_down
):
    seqs, length, width = tokens.shape
    dp, fsdp = lax.axis_size("dp"), lax.axis_size("fsdp")
    plan = Plan(dp, fsdp)
    me_d = lax.axis_index("dp")
    me = jnp.zeros((2,), jnp.int32)
    rows_all = seqs * length
    hidden_width = w_down.shape[0] * fsdp

    spread, pool, same = pooling(length)
    layout, _ = level_layout(length)
    local_rows = [first for level, first, _ in layout if 2 * NR * (1 << level) > length][0]
    spread_c = jnp.asarray(spread, BF16)
    pool_c = jnp.asarray(pool, BF16)
    same_c = jnp.asarray(same, F32)
    far_pool = jnp.asarray(pool[local_rows : local_rows + (length >> 4) + (length >> 5)], BF16)

    share = width // dp
    norms = jnp.stack([ln1_gain, ln1_bias, ln2_gain, ln2_bias])
    placed = lax.dynamic_update_slice(jnp.zeros((4, width), F32), norms, (0, me_d * share))
    placed = placed.reshape(4, 4, 128).transpose(1, 0, 2).reshape(LN_ROWS, 128)
    qkv_slots = gather(jnp.concatenate([w_qkv.T, placed], axis=0), plan)
    near, far_a, far_b = (swap(segments, m) for m in (1, 2, 3))
    bias = score_bias(segments, near, far_a, far_b)
    down_slots = gather(w_down.T, plan)
    out_slots = gather(w_out.T, plan)
    up_slots = gather(w_up.T, plan)

    tok = tokens.reshape(rows_all, width)
    cot = cotangent.reshape(rows_all, width)
    packed, wqh, wql, xhat1, inv1, ln, s4, s5 = qkv_stage(
        me, tok, qkv_slots, plan, far_pool, seqs
    )
    far = jnp.concatenate([swap(s4, 1), swap(s5, 2), swap(s5, 3)], axis=2)
    attended, lse = attention_forward(
        packed, far, bias, spread_c, pool_c, same_c, seqs, local_rows
    )
    middle, xhat2, inv2, oh, ol = middle_stage(me, tok, attended, out_slots, plan)
    gh, dh, dl = grad_hidden_stage(me, cot, down_slots, plan, hidden_width)
    hh, hl, ph, plo, uh, ul = hidden_stage(me, xhat2, ln, gh, up_slots, plan)
    g_down = reduce_pieces(grad_down_stage(me, cot, hh, hl, plan), plan)
    g_up = reduce_pieces(grad_up_stage(me, xhat2, ln, ph, plo, plan), plan)
    output, gm, gln = output_stage(
        middle, cot, xhat2, inv2, ln, hh, hl, ph, plo, dh, dl, uh, ul
    )
    gmix, out_pieces = mixture_grad_stage(me, gm, attended, oh, ol, plan)
    g_out = reduce_pieces(out_pieces, plan)
    dq, dk, dv, f4, f5a, f5b = attention_backward(
        packed, far, bias, spread_c, pool_c, same_c, attended, lse, gmix, seqs, local_rows
    )
    g4, g5a, g5b = swap(f4, 1), swap(f5a, 2), swap(f5b, 3)
    gph, gpl, gtok, lrow = input_grad_stage(
        dq, dk, dv, g4, g5a, g5b, far_pool, wqh, wql, xhat1, inv1, ln, gm, gln, seqs
    )
    g_qkv = reduce_pieces(grad_qkv_stage(me, gph, gpl, xhat1, ln, lrow, plan), plan)
    rows = g_qkv.shape[0] - LN_ROWS
    sums = g_qkv[rows:].reshape(4, 4, 128).transpose(1, 0, 2).reshape(4, width)
    mine = lax.dynamic_slice(sums, (0, me_d * share), (4, share))
    shape = tokens.shape
    return (
        output.reshape(shape),
        gtok.reshape(shape),
        mine[0],
        mine[1],
        g_qkv[:rows].T,
        g_out.T,
        mine[2],
        mine[3],
        g_up.T,
        g_down.T,
    )


def solution(mesh):
    weight = P("fsdp", "dp")
    rows = P("dp", "fsdp", None)
    vector = P("dp")
    return jax.shard_map(
        local,
        mesh=mesh,
        in_specs=(rows, P("dp", "fsdp"), rows, vector, vector, weight, weight, vector, vector, weight, weight),
        out_specs=(rows, rows, vector, vector, weight, weight, vector, vector, weight, weight),
        check_vma=False,
    )
```

time: 1670 us -> 906 us (0.54); the launches traced: 1650 us -> 905 us
  local copies, waits for them, and re-layouts: 673 us -> 26.4 us
  waiting for transfers between devices: 307 us -> 721 us
  matrix products: 278 us -> 0 us
  other arithmetic: 255 us -> 3.52 us
  Pallas kernels: 0 us -> 132 us
  blocking collectives: 110 us -> 0 us
    broadcast_in_dim x268 -> x11, local copies, waits for them, and re-layouts: 281 us -> 0.78 us  [the longest x5 0.39 us: score_bias(): low_q = jnp.repeat(low_q, ratio, axis=1)]
    dot_general x104 -> x0, matrix products: 278 us -> none  [the longest x30 69.9 us: block_part(): jnp.einsum('gbhij,gbjhd->gbihd', probabilities, val_b, precision=HIGHEST)]
    reduce_scatter x12 -> x4, waiting for transfers between devices: 306 us -> 525 us  [reduce_pieces(): lax.psum_scatter(flat, ('dp', 'fsdp'), scatter_dimension=0, tiled=False)]
    all_gather x4, waiting for transfers between devices: 0.01 us -> 185 us  [gather(): out = lax.all_gather(piece, ('dp', 'fsdp'), axis=0, tiled=False)]
    pallas_call x0 -> x12, Pallas kernels: none -> 132 us  [the longest x1 29.5 us: attention_backward(): pl.pallas_call(body, grid=(seqs, width // 128), out_shape=[jax.ShapeDtype...]
    reduce_sum x87 -> x0, other arithmetic: 129 us -> none  [the longest x30 62.7 us: expand(): return jnp.repeat(values, group_ratio, axis=1)]
    reshape x120 -> x9, local copies, waits for them, and re-layouts: 119 us -> 9.86 us  [the longest x1 5.67 us: reduce_pieces(): flat = pieces.reshape((plan.dp * plan.fsdp,) + pieces.shape[2:])]
    all_gather x9 -> x0, blocking collectives: 60.8 us -> none  [the longest x2 11.8 us: local(): lax.all_gather(send_k, 'fsdp', axis=1, tiled=True)]
  transfers between devices with their start and end apart: 16 -> 17, of which waited for: 6 -> 11; matrix products, arithmetic and copies ran while one was open for 47% -> 2% of each run, Pallas kernels for 0% -> 6%
where the time goes in v1:
time: 906 us; the launch traced here: 905 us
  waiting for transfers between devices  721 us (80%)
  Pallas kernels  132 us (15%)
  local copies, waits for them, and re-layouts  26.4 us (3%)
  between operations  14.4 us (2%)
    reduce_scatter x4, waiting for transfers between devices, reduce_pieces(): lax.psum_scatter(flat, ('dp', 'fsdp'), scatter_dimension=0, tiled=False)  525 us
    all_gather x4, waiting for transfers between devices, gather(): out = lax.all_gather(piece, ('dp', 'fsdp'), axis=0, tiled=False)  185 us
    pallas_call x1, Pallas kernels, attention_backward(): pl.pallas_call(body, grid=(seqs, width // 128), out_shape=[jax.ShapeDtype...  29.5 us
    pallas_call x1, Pallas kernels, attention_forward(): pl.pallas_call(body, grid=(seqs, width // 128), out_shape=[jax.ShapeDtype...  19.2 us
  transfers between devices with their start and end apart: 17, of which 11 were waited for; matrix products, arithmetic and copies ran while one was open for 2% of the time, Pallas kernels for 6%

profile of v1, /device:TPU:0, one launch (start us, length us, event | category | flops | bytes accessed | tf_op | source)
XLA Modules:
  0.0 905.1 jit_solution(14695781341415523607)
XLA Ops:
  7.3 0.7 pad_maximum_fusion.1
  8.2 1.5 pad_maximum_fusion
  9.8 0.7 all-gather.11.cloned.1.call-update
  10.5 0.7 all-gather.13.cloned.1.call-update
  11.3 0.5 all-gather.15.cloned.1.call-update
  11.8 0.5 collective-permute-start.3
  12.4 2.6 collective-permute-start.5
  15.1 0.8 reshape.129
  15.9 0.8 reshape.127
  16.6 0.8 reshape.126
  17.4 0.8 reshape.125
  18.2 0.8 reshape.124
  19.6 0.9 copy.86
  24.9 49.1 %all-gather.9.cloned.1.call-done = f32[6656,128]{1,0:T(8,128)} async-done(((f32[208,128]{1,0:T(8,128)}), f32[6656,128]{1,0:T(8,128)}) %all-gather.9.cloned.1.call-update) | async-done | bytes 3407888 | tf_op jit(solution)/shard_map/all_gather | solution.py:710
  74.6 7.4 shard_map.276
  82.5 1.5 concatenate.19.bias_ref
  83.9 1.3 collective-permute-start.2
  85.2 0.6 collective-permute-start.1
  85.8 4.1 collective-permute-done.1
  90.0 0.7 copy-done
  90.7 19.2 %shard_map.277 = (f32[512,512]{1,0:T(8,128)}, f32[512,512]{1,0:T(8,128)}) custom-call(f32[512,1536]{1,0:T(8,128)} %get-tuple-element.49.q_ref.k_ref.v_ref, f32[512,1536]{1,0:T(8,128)} %get-tuple-element.49.q_ref.k_ref.v_ref, f32[512,1536]{1,0:T(8,128)} %get-tuple-element.49.q_ref.k_ref.v_ref, f32[2,2,32,512]{3,2,1,0:T(8,128)} %copy-done, ...), custom_call_target="tpu_custom_call" | custom-call | tf_op jit(solution)/shard_map/pallas_call | solution.py:258
  109.9 19.9 %all-gather.11.cloned.1.call-done = f32[2048,128]{1,0:T(8,128)} async-done(((f32[64,128]{1,0:T(8,128)}), f32[2048,128]{1,0:T(8,128)}) %all-gather.11.cloned.1.call-update) | async-done | bytes 1048592 | tf_op jit(solution)/shard_map/all_gather | solution.py:710
  129.7 4.4 shard_map.278
  134.2 59.4 %all-gather.13.cloned.1.call-done = f32[2048,512]{1,0:T(8,128)} async-done(((f32[64,512]{1,0:T(8,128)}), f32[2048,512]{1,0:T(8,128)}) %all-gather.13.cloned.1.call-update) | async-done | bytes 4194320 | tf_op jit(solution)/shard_map/all_gather | solution.py:710
  193.5 8.3 shard_map.279
  201.8 57.1 %all-gather.15.cloned.1.call-done = f32[8192,128]{0,1:T(8,128)} async-done(((f32[256,128]{0,1:T(8,128)}), f32[8192,128]{0,1:T(8,128)}) %all-gather.15.cloned.1.call-update) | async-done | bytes 4194320 | tf_op jit(solution)/shard_map/all_gather | solution.py:710
  258.9 5.7 copy.71
  264.5 13.8 %shard_map.280 = (bf16[512,2048]{1,0:T(8,128)(2,1)}, bf16[512,2048]{1,0:T(8,128)(2,1)}, bf16[512,2048]{1,0:T(8,128)(2,1)}, bf16[512,2048]{1,0:T(8,128)(2,1)}, bf...) custom-call(s32[2]{0:T(128)} %broadcast_2_me_ref.2.me_ref, f32[512,512]{1,0:T(8,128)} %get-tuple-element.54.xhat_ref, ...), custom_call_target="tpu_custom_call" | custom-call | tf_op jit(solution)/shard_map/pallas_call | solution.py:481
  278.3 13.7 %shard_map.281 = (f32[512,512]{1,0:T(8,128)}, f32[512,512]{1,0:T(8,128)}, f32[8,512]{1,0:T(8,128)}) custom-call(f32[512,512]{1,0:T(8,128)} %get-tuple-element.53.mid, f32[512,512]{1,0:T(8,128)} %bitcast.69, f32[512,512]{1,0:T(8,128)} %get-tuple-element.54.xhat_ref, f32[512,128]{1,0:T(8,128)} %get-tuple-element.55.inv_ref, ...), custom_call_target="tpu_custom_call" | custom-call | tf_op jit(solution)/shard_map/pallas_call | solution.py:597
  292.1 4.9 shard_map.282
  296.9 29.5 %shard_map.283 = (f32[512,512]{1,0:T(8,128)}, f32[512,512]{1,0:T(8,128)}, f32[512,512]{1,0:T(8,128)}, f32[2,2,16,512]{3,2,1,0:T(8,128)}, f32[2,2,8,512]{3,2,1,0:T(8,128)}, /*index=5*/f32[2,2,8,512]{3,2,1,0:T(8,128)}) custom-call(f32[512,1536]{1,0:T(8,128)} %get-tuple-element.49.q_ref.k_ref.v_ref, f32[512,1536]{1,0:T(8,128)} %get-tuple-element.49.q_ref.k_ref.v_ref, ...), custom_call_target="tpu_custom_call" | custom-call | tf_op jit(solution)/shard_map/pallas_call | solution.py:357
  326.8 1.4 collective-permute-start.7
  328.4 2.9 collective-permute-done.7.g5a_r
  331.3 1.4 collective-permute-done.8.g5b_r
  332.7 0.6 copy-done.4
  333.4 8.2 shard_map.284
  341.5 6.6 shard_map.285
  348.2 0.5 reduce-scatter.7.cloned.1.call-update
  348.8 8.0 shard_map.287
  356.9 8.2 shard_map.286
  365.1 5.7 copy.72
  370.8 113.9 %reduce-scatter.5.cloned.1.call-done = f32[1,208,128]{2,1,0:T(8,128)} async-done(((f32[32,208,128]{2,1,0:T(8,128)}), f32[1,208,128]{2,1,0:T(8,128)}) %reduce-scatter.5.cloned.1.call-update) | async-done | bytes 106512 | tf_op jit(solution)/shard_map/reduce_scatter | solution.py:716
  484.7 0.7 slice.115
  485.4 0.5 slice_bitcast_fusion.1
  486.0 1.5 slice_bitcast_fusion
  487.5 130.7 %reduce-scatter.7.cloned.1.call-done = f32[1,64,128]{2,1,0:T(8,128)} async-done(((f32[32,64,128]{2,1,0:T(8,128)}), f32[1,64,128]{2,1,0:T(8,128)}) %reduce-scatter.7.cloned.1.call-update) | async-done | bytes 32784 | tf_op jit(solution)/shard_map/reduce_scatter | solution.py:716
  618.2 140.0 %reduce-scatter.11.cloned.1.call-done = f32[1,64,512]{2,1,0:T(8,128)} async-done(((f32[32,64,512]{2,1,0:T(8,128)}), f32[1,64,512]{2,1,0:T(8,128)}) %reduce-scatter.11.cloned.1.call-update) | async-done | bytes 131088 | tf_op jit(solution)/shard_map/reduce_scatter | solution.py:716
  758.2 140.0 %reduce-scatter.9.cloned.1.call-done = f32[1,256,128]{1,2,0:T(8,128)} async-done(((f32[32,256,128]{1,2,0:T(8,128)}), f32[1,256,128]{1,2,0:T(8,128)}) %reduce-scatter.9.cloned.1.call-update) | async-done | bytes 131088 | tf_op jit(solution)/shard_map/reduce_scatter | solution.py:716
  (93 shorter events, 7.2 us)
Async XLA Ops:
  7.2 14.6 %copy-start.7 = (pred[256,128]{1,0:T(32,128)(4,1)S(1)}, pred[256,128]{1,0:T(32,128)(4,1)}, u32[]{:S(2)}) copy-start(pred[256,128]{1,0:T(32,128)(4,1)} %constant.59) | copy-start | bytes 98308
  7.2 14.8 %copy-start.6 = (pred[256,64]{1,0:T(32,128)(4,1)S(1)}, pred[256,64]{1,0:T(32,128)(4,1)}, u32[]{:S(2)}) copy-start(pred[256,64]{1,0:T(32,128)(4,1)} %constant.60) | copy-start | bytes 49156
  7.2 15.0 %copy-start.5 = (pred[256,32]{1,0:T(32,128)(4,1)S(1)}, pred[256,32]{1,0:T(32,128)(4,1)}, u32[]{:S(2)}) copy-start(pred[256,32]{1,0:T(32,128)(4,1)} %constant.61) | copy-start | bytes 24580
  7.2 15.2 %copy-start.2 = (s32[2,256]{1,0:T(2,128)S(1)}, s32[2,256]{1,0:T(2,128)}, u32[]{:S(2)}) copy-start(s32[2,256]{1,0:T(2,128)} %param.22) | copy-start | bytes 6148
  7.2 66.8 %all-gather.9.cloned.1.call-start = ((), (), s32[]{:S(2)}) async-start(), calls=%async_computation.8 | async-start | bytes 3514368 | tf_op jit(solution)/shard_map/all_gather | solution.py:710
  9.7 120.0 %all-gather.11.cloned.1.call-start = ((), (), s32[]{:S(2)}) async-start(), calls=%async_computation.9 | async-start | bytes 1081344 | tf_op jit(solution)/shard_map/all_gather | solution.py:710
  10.5 183.1 %all-gather.13.cloned.1.call-start = ((), (), s32[]{:S(2)}) async-start(), calls=%async_computation.10 | async-start | bytes 4325376 | tf_op jit(solution)/shard_map/all_gather | solution.py:710
  11.2 247.7 %all-gather.15.cloned.1.call-start = ((), (), s32[]{:S(2)}) async-start(), calls=%async_computation.11 | async-start | bytes 4325376 | tf_op jit(solution)/shard_map/all_gather | solution.py:710
  11.8 472.9 %reduce-scatter.5.cloned.1.call-start = ((), (), s32[]{:S(2)}) async-start(), calls=%async_computation.4 | async-start | bytes 3514368 | tf_op jit(solution)/shard_map/reduce_scatter | solution.py:716
  11.8 12.5 %collective-permute-start.3 = (s32[2,256]{1,0:T(2,128)}, s32[2,256]{1,0:T(2,128)S(1)}, u32[]{:S(2)}, u32[]{:S(2)}) collective-permute-start(s32[2,256]{1,0:T(2,128)} %param.22), channel_id=1, source_target_pairs={{0,1},{1,0},{2,3},{3,2},{4,5},{5,4},{6,7},{7,6},{8,9},{9,8},{10,11... | collective-permute-start | bytes 6152 | tf_op jit(solution)/shard_map/ppermute | solution.py:706
  12.4 11.3 %collective-permute-start.5 = (s32[2,256]{1,0:T(2,128)}, s32[2,256]{1,0:T(2,128)S(1)}, u32[]{:S(2)}, u32[]{:S(2)}) collective-permute-start(s32[2,256]{1,0:T(2,128)} %param.22), channel_id=1, source_target_pairs={{0,3},{1,2},{2,1},{3,0},{4,7},{5,6},{6,5},{7,4},{8,11},{9,10},{10,... | collective-permute-start | bytes 6152 | tf_op jit(solution)/shard_map/ppermute | solution.py:706
  15.0 8.7 collective-permute-start.4
  81.9 2.0 copy-start.8
  81.9 3.9 collective-permute-start
  83.9 6.0 collective-permute-start.2
  85.2 4.7 collective-permute-start.1
  90.0 0.7 copy-start
  326.4 6.3 collective-permute-start.6
  326.8 4.5 collective-permute-start.7
  328.2 4.5 collective-permute-start.8
  331.3 1.4 copy-start.3
  332.7 0.6 copy-start.4
  332.7 0.7 copy-start.1
  348.2 270.0 %reduce-scatter.7.cloned.1.call-start = ((), (), s32[]{:S(2)}) async-start(), calls=%async_computation.5 | async-start | bytes 1081344 | tf_op jit(solution)/shard_map/reduce_scatter | solution.py:716
  348.8 409.5 %reduce-scatter.11.cloned.1.call-start = ((), (), s32[]{:S(2)}) async-start(), calls=%async_computation.7 | async-start | bytes 4325376 | tf_op jit(solution)/shard_map/reduce_scatter | solution.py:716
  356.8 541.4 %reduce-scatter.9.cloned.1.call-start = ((), (), s32[]{:S(2)}) async-start(), calls=%async_computation.6 | async-start | bytes 4325376 | tf_op jit(solution)/shard_map/reduce_scatter | solution.py:716
Sparse Core Ops, SparseCore 0:
  11.5 62.5 all-gather.8
  76.9 52.7 all-gather.10
  132.6 60.8 all-gather.12
  196.3 62.5 all-gather.14
  348.3 136.3 reduce-scatter.4
  487.4 130.7 reduce-scatter.6
  621.1 137.0 reduce-scatter.10
  761.1 137.1 reduce-scatter.8
